TPU v7x, 32 devices: a whole 2x2x4 slice. The times are simulated.
32 devices in a mesh: dp: 8 (over y, x, core), mp: 4 (over z).
Axes of the slice: x: 2, y: 2, z: 4, core: 2. Of those that a mesh axis runs over, the one named last changes fastest.
Arguments:
- tokens_in: bfloat16 [16384, 768], P(('dp', 'mp')), may hold values from -5 to 5
- timesteps: int32 [8], replicated, may hold values from 0 to 999
- lengths: int32 [8], replicated, may hold values from 512 to 2048, as said below
- time_table: bfloat16 [1000, 768], replicated, may hold values from -0.8984375 to 0.8984375
- norm_gains: float32 [2, 768], replicated, may hold values from 0.5 to 1.5
- norm_biases: float32 [2, 768], replicated, may hold values from -0.6 to 0.6
- w_qkv: bfloat16 [3, 768, 768], P(None, 'dp', 'mp'), may hold values from -0.3125 to 0.3125
- qv_bias: float32 [2, 768], replicated, may hold values from -0.42 to 0.42
- w_out: bfloat16 [768, 768], P('mp', 'dp'), may hold values from -0.21875 to 0.21875
- out_bias: float32 [768], replicated, may hold values from -0.6 to 0.6
- w_up: bfloat16 [768, 3072], P('dp', 'mp'), may hold values from -0.21875 to 0.21875
- up_bias: float32 [3072], replicated, may hold values from -0.8 to 0
- w_down: bfloat16 [3072, 768], P('mp', 'dp'), may hold values from -0.109375 to 0.109375
- down_bias: float32 [768], replicated, may hold values from -0.6 to 0.6
- cotangent: bfloat16 [16384, 768], P(('dp', 'mp')), may hold values from -50 to 50
- teacher: bfloat16 [16384, 768], P(('dp', 'mp')), may hold values from -5 to 5
Outputs:
- output: bfloat16 [16384, 768], P(('dp', 'mp'))
- input_grad: float32 [16384, 768], P(('dp', 'mp'))
- table_grad: float32 [1000, 768], replicated
- norm_gain_grad: float32 [2, 768], replicated
- norm_bias_grad: float32 [2, 768], replicated
- w_qkv_grad: float32 [3, 768, 768], P(None, 'dp', 'mp')
- qv_bias_grad: float32 [2, 768], replicated
- w_out_grad: float32 [768, 768], P('mp', 'dp')
- out_bias_grad: float32 [768], replicated
- w_up_grad: float32 [768, 3072], P('dp', 'mp')
- up_bias_grad: float32 [3072], replicated
- w_down_grad: float32 [3072, 768], P('mp', 'dp')
- down_bias_grad: float32 [768], replicated
Inputs may be any that keep to these rules, and one draw needn't show every extreme that they name: Sequence s holds its valid tokens in its first lengths[s] slots and padding after them; some sequence fills all 2048 slots.
All inputs are finite; a program needn't handle non-finite values.
Results may differ from a plain program's by a relative error of at most 0.0095.
The roundings to bfloat16 on the way count: a program that leaves them out, or rounds other values in their place, can miss the bound.
Values may be sent and summed in bfloat16 or wider, within the bound.
No kernel may reach another device: no remote copies, remote signals or barrier semaphores. Data moves between devices by JAX's collectives and lax.ppermute only.
A program may use at most 128 MiB of HBM per device.

v0:
```python
import jax
import jax.numpy as jnp
from jax import lax
from jax.sharding import PartitionSpec as P

D = 768
HEAD_DIM = 64
FF = 3072
MAXLEN = 2048
SEQ_DEV = 1
far_below = -1e30
epsilon = 1e-05


def norm_rows(values, gain_row, shift_row):
    center = values - jnp.mean(values, axis=-1, keepdims=True)
    spread = jnp.mean(center * center, axis=-1, keepdims=True)
    return center * lax.rsqrt(spread + epsilon) * gain_row + shift_row


def gelu_exact(values):
    return jax.nn.gelu(values, approximate=False)


def contract_rows(left_side, right_side):
    return lax.dot_general(
        left_side, right_side, (((0,), (0,)), ((), ())), preferred_element_type=jnp.float32
    )


def contract_cols(left_side, right_side):
    return lax.dot_general(
        left_side, right_side, (((1,), (1,)), ((), ())), preferred_element_type=jnp.float32
    )


def exact_rows(left_side, right_side):
    return lax.dot_general(
        left_side,
        right_side,
        (((0,), (0,)), ((), ())),
        precision=lax.Precision.HIGHEST,
        preferred_element_type=jnp.float32,
    )


def attend_forward(queries, keys_seq, values_seq, length, block_rows, score_scale):
    blocks = queries.shape[0] // block_rows
    key_kept = jnp.arange(keys_seq.shape[0]) < length
    query_blocks = queries.reshape((blocks, block_rows) + queries.shape[1:])

    def one_block(query_block):
        scores = (
            jnp.einsum("qhd,khd->hqk", query_block, keys_seq, preferred_element_type=jnp.float32)
            * score_scale
        )
        scores = jnp.where(key_kept[None, None, :], scores, far_below)
        highest = jnp.max(scores, axis=-1, keepdims=True)
        exp_scores = jnp.exp(scores - highest)
        totals = jnp.sum(exp_scores, axis=-1, keepdims=True)
        prob_low = (exp_scores / totals).astype(jnp.bfloat16)
        mixed_rows = jnp.einsum(
            "hqk,khd->qhd", prob_low, values_seq, preferred_element_type=jnp.float32
        )
        return (mixed_rows, (highest + jnp.log(totals))[..., 0])

    mixed_rows, log_totals = lax.map(one_block, query_blocks)
    return (mixed_rows.reshape(queries.shape), log_totals)


def attend_backward(
    queries, keys_seq, values_seq, grads_out, log_totals, length, block_rows, score_scale
):
    blocks = queries.shape[0] // block_rows
    key_kept = jnp.arange(keys_seq.shape[0]) < length
    query_blocks = queries.reshape((blocks, block_rows) + queries.shape[1:])
    grad_blocks = grads_out.reshape((blocks, block_rows) + grads_out.shape[1:])

    def one_block(carried, inputs):
        key_grad, value_grad = carried
        query_block, grad_block, log_block = inputs
        scores = (
            jnp.einsum("qhd,khd->hqk", query_block, keys_seq, preferred_element_type=jnp.float32)
            * score_scale
        )
        scores = jnp.where(key_kept[None, None, :], scores, far_below)
        prob_rows = jnp.exp(scores - log_block[..., None])
        value_grad = value_grad + jnp.einsum(
            "hqk,qhd->khd",
            prob_rows.astype(jnp.bfloat16),
            grad_block,
            preferred_element_type=jnp.float32,
        )
        prob_grad = jnp.einsum(
            "qhd,khd->hqk", grad_block, values_seq, preferred_element_type=jnp.float32
        )
        score_grad = (
            prob_rows * (prob_grad - jnp.sum(prob_rows * prob_grad, axis=-1, keepdims=True))
        ).astype(jnp.bfloat16)
        query_grad = (
            jnp.einsum("hqk,khd->qhd", score_grad, keys_seq, preferred_element_type=jnp.float32)
            * score_scale
        )
        key_grad = (
            key_grad
            + jnp.einsum(
                "hqk,qhd->khd", score_grad, query_block, preferred_element_type=jnp.float32
            )
            * score_scale
        )
        return ((key_grad, value_grad), query_grad)

    empty_grad = jnp.zeros(keys_seq.shape, jnp.float32)
    (key_grad, value_grad), query_grad = lax.scan(
        one_block, (empty_grad, empty_grad), (query_blocks, grad_blocks, log_totals)
    )
    return (query_grad.reshape(queries.shape), key_grad, value_grad)


def shards(
    tokens_in,
    timesteps,
    lengths,
    time_table,
    norm_gains,
    norm_biases,
    w_qkv,
    qv_bias,
    w_out,
    out_bias,
    w_up,
    up_bias,
    w_down,
    down_bias,
    cotangent,
    teacher,
):
    model_rank = lax.axis_index("mp")
    data_rank = lax.axis_index("dp")
    model_count = lax.axis_size("mp")
    own_rows = tokens_in.shape[0]
    group_rows = own_rows * model_count
    local_width = w_qkv.shape[2]
    local_hidden = w_up.shape[1]
    local_heads = local_width // HEAD_DIM
    block_rows = min(512, MAXLEN)
    score_scale = HEAD_DIM ** (-0.5)
    group_lengths = lax.dynamic_slice_in_dim(lengths, data_rank * SEQ_DEV, SEQ_DEV)
    group_times = lax.dynamic_slice_in_dim(timesteps, data_rank * SEQ_DEV, SEQ_DEV)
    row_index = model_rank * own_rows + jnp.arange(own_rows)
    row_member = (row_index // MAXLEN)[:, None] == jnp.arange(SEQ_DEV)[None, :]
    row_length = jnp.sum(jnp.where(row_member, group_lengths[None, :], 0), axis=1)
    row_time = jnp.sum(jnp.where(row_member, group_times[None, :], 0), axis=1)
    row_valid = row_index % MAXLEN < row_length
    time_onehot = row_time[:, None] == jnp.arange(time_table.shape[0])[None, :]
    table_rows = jnp.dot(
        time_onehot.astype(jnp.bfloat16), time_table, preferred_element_type=jnp.float32
    )
    start_state = tokens_in.astype(jnp.float32) + table_rows
    qkv_weight, out_weight, up_weight, down_weight = (
        lax.all_gather(w_qkv, "dp", axis=1, tiled=True),
        lax.all_gather(w_out, "dp", axis=1, tiled=True),
        lax.all_gather(w_up, "dp", axis=0, tiled=True),
        lax.all_gather(w_down, "dp", axis=1, tiled=True),
    )
    first_norm = norm_rows(start_state, norm_gains[0], norm_biases[0]).astype(jnp.bfloat16)
    first_all = lax.all_gather(first_norm, "mp", axis=0, tiled=True)
    width_start = model_rank * local_width
    local_bias = lax.dynamic_slice_in_dim(qv_bias, width_start, local_width, 1)
    bias_stack = jnp.stack([local_bias[0], jnp.zeros_like(local_bias[0]), local_bias[1]])
    projected = jnp.einsum("gd,cde->cge", first_all, qkv_weight, preferred_element_type=jnp.float32)
    projected = (projected + bias_stack[:, None, :]).astype(jnp.bfloat16)
    heads_all = projected.reshape(3, SEQ_DEV, MAXLEN, local_heads, HEAD_DIM)
    member = 0
    mixed_seq, log_seq = attend_forward(
        heads_all[0, member],
        heads_all[1, member],
        heads_all[2, member],
        group_lengths[member],
        block_rows,
        score_scale,
    )
    mixed_parts = [mixed_seq]
    log_parts = [log_seq]
    attended = jnp.stack(mixed_parts).reshape(group_rows, local_width).astype(jnp.bfloat16)
    attn_sum = lax.psum_scatter(
        jnp.dot(attended, out_weight, preferred_element_type=jnp.float32),
        "mp",
        scatter_dimension=0,
        tiled=True,
    )
    middle_state = start_state + attn_sum + out_bias
    second_norm = norm_rows(middle_state, norm_gains[1], norm_biases[1]).astype(jnp.bfloat16)
    second_all = lax.all_gather(second_norm, "mp", axis=0, tiled=True)
    hidden_start = model_rank * local_hidden
    hidden_pre = jnp.dot(
        second_all, up_weight, preferred_element_type=jnp.float32
    ) + lax.dynamic_slice_in_dim(up_bias, hidden_start, local_hidden)
    hidden_act = gelu_exact(hidden_pre).astype(jnp.bfloat16)
    ffn_sum = lax.psum_scatter(
        jnp.dot(hidden_act, down_weight, preferred_element_type=jnp.float32),
        "mp",
        scatter_dimension=0,
        tiled=True,
    )
    final_state = middle_state + ffn_sum + down_bias
    output = final_state.astype(jnp.bfloat16)
    valid_total = jnp.sum(lengths).astype(jnp.float32)
    loss_weight = lengths.shape[0] * MAXLEN / valid_total
    final_grad = jnp.where(
        row_valid[:, None],
        cotangent.astype(jnp.float32) + loss_weight * (final_state - teacher.astype(jnp.float32)),
        0.0,
    )
    final_low = final_grad.astype(jnp.bfloat16)
    _, gelu_back = jax.vjp(gelu_exact, hidden_pre)
    final_all = lax.all_gather(final_low, "mp", axis=0, tiled=True)
    down_grad_part = contract_rows(hidden_act, final_all)
    act_grad = contract_cols(final_all, down_weight)
    pre_grad = gelu_back(act_grad)[0].astype(jnp.bfloat16)
    up_grad_part = contract_rows(second_all, pre_grad)
    up_bias_part = lax.dynamic_update_slice_in_dim(
        jnp.zeros((FF,), jnp.float32), jnp.sum(pre_grad, axis=0, dtype=jnp.float32), hidden_start, 0
    )
    second_grad = lax.psum_scatter(
        contract_cols(pre_grad, up_weight), "mp", scatter_dimension=0, tiled=True
    )
    _, second_back = jax.vjp(norm_rows, middle_state, norm_gains[1], norm_biases[1])
    middle_part, gain_two, shift_two = second_back(second_grad)
    middle_grad = final_grad + middle_part
    middle_all = lax.all_gather(middle_grad.astype(jnp.bfloat16), "mp", axis=0, tiled=True)
    out_grad_part = contract_rows(attended, middle_all)
    attended_grad = contract_cols(middle_all, out_weight).astype(jnp.bfloat16)
    grad_heads = attended_grad.reshape(SEQ_DEV, MAXLEN, local_heads, HEAD_DIM)
    member = 0
    query_grad, key_grad, value_grad = attend_backward(
        heads_all[0, member],
        heads_all[1, member],
        heads_all[2, member],
        grad_heads[member],
        log_parts[member],
        group_lengths[member],
        block_rows,
        score_scale,
    )
    query_grads = [query_grad]
    key_grads = [key_grad]
    value_grads = [value_grad]
    projected_grad = jnp.stack(
        [jnp.stack(query_grads), jnp.stack(key_grads), jnp.stack(value_grads)]
    )
    projected_grad = projected_grad.reshape(3, group_rows, local_width).astype(jnp.bfloat16)
    qkv_grad_part = jnp.einsum(
        "gd,cge->cde", first_all, projected_grad, preferred_element_type=jnp.float32
    )
    bias_sums = jnp.sum(projected_grad, axis=1, dtype=jnp.float32)
    qv_bias_part = lax.dynamic_update_slice_in_dim(
        jnp.zeros((2, D), jnp.float32), jnp.stack([bias_sums[0], bias_sums[2]]), width_start, 1
    )
    first_grad = lax.psum_scatter(
        jnp.einsum("cge,cde->gd", projected_grad, qkv_weight, preferred_element_type=jnp.float32),
        "mp",
        scatter_dimension=0,
        tiled=True,
    )
    _, first_back = jax.vjp(norm_rows, start_state, norm_gains[0], norm_biases[0])
    start_part, gain_one, shift_one = first_back(first_grad)
    input_grad = middle_grad + start_part
    qkv_grad, out_grad, up_grad, down_grad = (
        lax.psum_scatter(qkv_grad_part, "dp", scatter_dimension=1, tiled=True),
        lax.psum_scatter(out_grad_part, "dp", scatter_dimension=1, tiled=True),
        lax.psum_scatter(up_grad_part, "dp", scatter_dimension=0, tiled=True),
        lax.psum_scatter(down_grad_part, "dp", scatter_dimension=1, tiled=True),
    )
    vector_part = jnp.stack(
        [
            gain_one,
            gain_two,
            shift_one,
            shift_two,
            qv_bias_part[0],
            qv_bias_part[1],
            jnp.sum(middle_grad, axis=0),
            jnp.sum(final_grad, axis=0),
        ]
    )
    table_part = exact_rows(time_onehot.astype(jnp.float32), input_grad)
    vector_sum, up_bias_grad, table_grad = lax.psum(
        (vector_part, up_bias_part, table_part), ("dp", "mp")
    )
    return (
        output,
        input_grad,
        table_grad,
        vector_sum[0:2],
        vector_sum[2:4],
        qkv_grad,
        vector_sum[4:6],
        out_grad,
        vector_sum[6],
        up_grad,
        up_bias_grad,
        down_grad,
        vector_sum[7],
    )


def solution(mesh):
    placed = (
        P(("dp", "mp"), None),
        P(),
        P(),
        P(),
        P(),
        P(),
        P(None, "dp", "mp"),
        P(),
        P("mp", "dp"),
        P(),
        P("dp", "mp"),
        P(),
        P("mp", "dp"),
        P(),
        P(("dp", "mp"), None),
        P(("dp", "mp"), None),
    )
    return jax.shard_map(
        shards,
        mesh=mesh,
        in_specs=placed,
        out_specs=(
            P(("dp", "mp"), None),
            P(("dp", "mp"), None),
            P(),
            P(),
            P(),
            P(None, "dp", "mp"),
            P(),
            P("mp", "dp"),
            P(),
            P("dp", "mp"),
            P(),
            P("mp", "dp"),
            P(),
        ),
        check_vma=False,
    )
```

profile of v0, /device:TPU:0, one launch (start us, length us, event | category | flops | bytes accessed | tf_op | source)
XLA Modules:
  0.0 1150.8 jit_solution(8117117334112619755)
XLA Ops:
  17.3 14.6 %all_gather.25 = bf16[3,768,192]{2,0,1:T(4,128)(2,1)S(1)} all-gather(bf16[3,96,192]{2,0,1:T(4,128)(2,1)S(1)} %copy.44), channel_id=1, replica_groups=mesh['dp'=8,'mp'=4] {'dp'}, dimensions={1}, use_global_device_ids=true | all-gather | bytes 995328 | tf_op jit(solution)/shard_map/all_gather | solution.py:161
  34.1 8.7 all_gather.26
  43.7 39.0 %all-gather.7.cloned.1.call-done = bf16[2048,768]{1,0:T(8,128)(2,1)} async-done(((bf16[512,768]{1,0:T(8,128)(2,1)}), bf16[2048,768]{1,0:T(8,128)(2,1)}) %all-gather.7.cloned.1.call-update) | async-done | bytes 3145744 | tf_op jit(solution)/shard_map/all_gather | solution.py:167
  91.1 40.3 %while.28 = (s32[]{:T(128)}, bf16[4,512,3,64]{1,3,2,0:T(8,128)(2,1)}, f32[4,3,512]{2,1,0:T(4,128)S(1)}, bf16[4,512,3,64]{1,3,2,0:T(8,128)(2,1)S(1)}, bf16[2048,3...) while((s32[]{:T(128)}, ...), condition=%wide.region_5.6_spmd.clone, body=%wide.region_2.5_spmd.clone.sunk | while | flops 843055616 | bytes 46270628 | solution.py:67
  139.1 108.9 %reduce-scatter.13.cloned.1.call-done = f32[512,768]{1,0:T(8,128)} async-done(((f32[2048,768]{1,0:T(8,128)}), f32[512,768]{1,0:T(8,128)}) %reduce-scatter.13.cloned.1.call-update) | async-done | bytes 1572880 | tf_op jit(solution)/shard_map/reduce_scatter | solution.py:186
  253.4 62.4 %all-gather.9.cloned.1.call-done = bf16[2048,768]{1,0:T(8,128)(2,1)} async-done(((bf16[512,768]{1,0:T(8,128)(2,1)}), bf16[2048,768]{1,0:T(8,128)(2,1)}) %all-gather.9.cloned.1.call-update) | async-done | bytes 3145744 | tf_op jit(solution)/shard_map/all_gather | solution.py:194
  315.7 18.9 %multiply_convert_fusion.1 = (bf16[2048,768]{1,0:T(8,128)(2,1)}, f32[2048,768]{1,0:T(8,128)}, f32[2048,768]{1,0:T(8,128)}) fusion(f32[768]{0:T(1024)S(1)} %dynamic_slice.29, bf16[2048,768]{1,0:T(8,128)(2,1)} %all-gather.9.cloned.1.call-done, bf16[768,768]{1,0:T(8,128)(2,1)} %all-gather.11.cloned.1.call-done), kind=kOutput, calls=%fused_computation.54 | convolution fusion | flops 2519728128 | bytes 20057088 | tf_op jit(solution)/shard_map/dot_general | solution.py:196
  334.7 5.4 all-gather.13.cloned.1.call-done
  340.1 7.5 fusion.81
  350.2 108.2 %reduce-scatter.15.cloned.1.call-done = f32[512,768]{1,0:T(8,128)} async-done(((f32[2048,768]{1,0:T(8,128)}), f32[512,768]{1,0:T(8,128)}) %reduce-scatter.15.cloned.1.call-update) | async-done | bytes 1572880 | tf_op jit(solution)/shard_map/reduce_scatter | solution.py:200
  464.8 63.7 %all-gather.15.cloned.1.call-done = bf16[2048,768]{1,0:T(8,128)(2,1)} async-done(((bf16[512,768]{1,0:T(8,128)(2,1)}), bf16[2048,768]{1,0:T(8,128)(2,1)}) %all-gather.15.cloned.1.call-update) | async-done | bytes 3145744 | tf_op jit(solution)/shard_map/all_gather | solution.py:217
  528.5 11.1 convert_reduce_fusion
  545.9 109.4 %reduce-scatter.17.cloned.1.call-done = f32[512,768]{1,0:T(8,128)} async-done(((f32[2048,768]{1,0:T(8,128)}), f32[512,768]{1,0:T(8,128)}) %reduce-scatter.17.cloned.1.call-update) | async-done | bytes 1572880 | tf_op jit(solution)/shard_map/reduce_scatter | solution.py:225
  662.5 64.1 %all-gather.17.cloned.1.call-done = bf16[2048,768]{1,0:T(8,128)(2,1)} async-done(((bf16[512,768]{1,0:T(8,128)(2,1)}), bf16[2048,768]{1,0:T(8,128)(2,1)}) %all-gather.17.cloned.1.call-update) | async-done | bytes 3145744 | tf_op jit(solution)/shard_map/all_gather | solution.py:231
  736.7 105.6 %while.29 = (s32[]{:T(128)}, f32[2048,3,64]{0,2,1:T(8,128)S(1)}, f32[2048,3,64]{0,2,1:T(8,128)}, bf16[4,512,3,64]{1,3,2,0:T(8,128)(2,1)}, bf16[4,512,3,64]{1,3,2...) while((s32[]{:T(128)}, f32[2048,3,64]{0,2,1:T(8,128)S(1)}, ...), condition=%wide.region_16.17_spmd.clone, body=%wide.region_14.16_spmd.clone.sunk | while | flops 2062516736 | bytes 129419448 | solution.py:114
  740.3 4.9 fusion.149
  754.7 5.6 fusion.150
  766.2 5.5 fusion.149
  781.2 5.6 fusion.150
  792.6 5.4 fusion.149
  807.7 5.6 fusion.150
  819.1 5.5 fusion.149
  829.3 4.8 multiply_convert_fusion.3
  834.1 5.6 fusion.150
  858.4 5.7 fusion.56
  873.0 6.9 fusion.83
  880.2 6.9 fusion.84
  887.2 75.4 %reduce-scatter.19.cloned.1.call-done = f32[512,768]{1,0:T(8,128)} async-done(((f32[2048,768]{1,0:T(8,128)}), f32[512,768]{1,0:T(8,128)}) %reduce-scatter.19.cloned.1.call-update) | async-done | bytes 1572880 | tf_op jit(solution)/shard_map/reduce_scatter | solution.py:260
  973.6 28.2 %reduce-scatter.27.cloned.1.call-done = f32[96,192]{1,0:T(8,128)} async-done(((f32[768,192]{1,0:T(8,128)}), f32[96,192]{1,0:T(8,128)}) %reduce-scatter.27.cloned.1.call-update) | async-done | bytes 73744
  1003.4 42.7 %reduce-scatter.25.cloned.1.call-done = f32[96,576]{1,0:T(8,128)} async-done(((f32[768,576]{1,0:T(8,128)}), f32[96,576]{1,0:T(8,128)}) %reduce-scatter.25.cloned.1.call-update) | async-done | bytes 221200
  1048.1 40.7 %all-reduce = (f32[8,768]{1,0:T(8,128)S(1)}, f32[3072]{0:T(1024)}) all-reduce(f32[8,768]{1,0:T(8,128)S(1)} %stack.37, f32[3072]{0:T(1024)S(1)} %dynamic_update_slice.18), channel_id=1, replica_groups=mesh['dp'=8,'mp'=4] {'dp','mp'}, use_global_device_ids=true, to_apply=%region_28.29 | all-reduce | flops 9216 | bytes 73728 | tf_op jit(solution)/shard_map/psum | solution.py:288
  1092.9 46.9 %reduce-scatter.23.cloned.1.call-done = f32[768,96]{0,1:T(8,128)} async-done(((f32[768,768]{0,1:T(8,128)}), f32[768,96]{0,1:T(8,128)}) %reduce-scatter.23.cloned.1.call-update) | async-done | bytes 294928 | tf_op jit(solution)/shard_map/reduce_scatter | solution.py:273
  (273 shorter events, 209.3 us)
Async XLA Ops:
  8.0 74.7 %all-gather.7.cloned.1.call-start = ((), (), s32[]{:S(2)}) async-start(), calls=%async_computation.8 | async-start | bytes 3932160 | tf_op jit(solution)/shard_map/all_gather | solution.py:167
  8.9 5.5 copy-start.26
  16.3 231.7 %reduce-scatter.13.cloned.1.call-start = ((), (), s32[]{:S(2)}) async-start(), calls=%async_computation.9 | async-start | bytes 7864320 | tf_op jit(solution)/shard_map/reduce_scatter | solution.py:186
  131.3 7.1 copy-start.3
  131.3 7.1 copy-start.6
  138.5 109.6 %copy-start.41 = (f32[768]{0:T(1024)S(1)}, f32[768]{0:T(1024)}, u32[]{:S(2)}) copy-start(f32[768]{0:T(1024)} %param.29) | copy-start | bytes 9220
  138.5 114.9 %all-gather.11.cloned.1.call-start = ((), (), s32[]{:S(2)}) async-start(), calls=%async_computation.11 | async-start | bytes 1327104 | tf_op jit(solution)/shard_map/all_gather | solution.py:163
  139.1 176.7 %all-gather.9.cloned.1.call-start = ((), (), s32[]{:S(2)}) async-start(), calls=%async_computation.10 | async-start | bytes 3932160 | tf_op jit(solution)/shard_map/all_gather | solution.py:194
  251.8 88.3 %all-gather.13.cloned.1.call-start = ((), (), s32[]{:S(2)}) async-start(), calls=%async_computation.12 | async-start | bytes 1327104 | tf_op jit(solution)/shard_map/all_gather | solution.py:164
  252.3 206.0 %reduce-scatter.15.cloned.1.call-start = ((), (), s32[]{:S(2)}) async-start(), calls=%async_computation.13 | async-start | bytes 7864320 | tf_op jit(solution)/shard_map/reduce_scatter | solution.py:200
  347.5 110.8 %copy-start.42 = (f32[768]{0:T(1024)S(1)}, f32[768]{0:T(1024)}, u32[]{:S(2)}) copy-start(f32[768]{0:T(1024)} %param.33) | copy-start | bytes 9220
  347.6 180.9 %all-gather.15.cloned.1.call-start = ((), (), s32[]{:S(2)}) async-start(), calls=%async_computation.14 | async-start | bytes 3932160 | tf_op jit(solution)/shard_map/all_gather | solution.py:217
  464.3 190.9 %reduce-scatter.17.cloned.1.call-start = ((), (), s32[]{:S(2)}) async-start(), calls=%async_computation.15 | async-start | bytes 7864320 | tf_op jit(solution)/shard_map/reduce_scatter | solution.py:225
  528.5 12.8 %copy-start.44 = (bf16[768,768]{1,0:T(8,128)(2,1)S(1)}, bf16[768,768]{1,0:T(8,128)(2,1)}, u32[]{:S(2)}) copy-start(bf16[768,768]{1,0:T(8,128)(2,1)} %all-gather.11.cloned.1.call-done) | copy-start | bytes 3538948
  545.8 180.8 %all-gather.17.cloned.1.call-start = ((), (), s32[]{:S(2)}) async-start(), calls=%async_computation.16 | async-start | bytes 3932160 | tf_op jit(solution)/shard_map/all_gather | solution.py:231
  662.4 300.2 %reduce-scatter.19.cloned.1.call-start = ((), (), s32[]{:S(2)}) async-start(), calls=%async_computation.17 | async-start | bytes 7864320 | tf_op jit(solution)/shard_map/reduce_scatter | solution.py:260
  754.7 5.6 copy-start.2
  781.2 5.6 copy-start.2
  807.7 5.6 copy-start.2
  834.1 5.6 copy-start.2
  853.0 5.3 copy-start.19
  853.0 148.7 %reduce-scatter.27.cloned.1.call-start = ((), (), s32[]{:S(2)}) async-start(), calls=%async_computation.22 | async-start | bytes 884736
  858.3 187.8 %reduce-scatter.25.cloned.1.call-start = ((), (), s32[]{:S(2)}) async-start(), calls=%async_computation.21 | async-start | bytes 2211840
  872.9 219.9 %reduce-scatter.21.cloned.1.call-start = ((), (), s32[]{:S(2)}) async-start(), calls=%async_computation.19 | async-start | bytes 2654208 | tf_op jit(solution)/shard_map/reduce_scatter | solution.py:272
  879.9 82.7 %copy-start.27 = (f32[768]{0:T(1024)S(1)}, f32[768]{0:T(1024)}, u32[]{:S(2)}) copy-start(f32[768]{0:T(1024)} %copy-done.26) | copy-start | bytes 9220
  879.9 82.7 %copy-start.29 = (f32[512]{0:T(512)S(1)}, f32[512]{0:T(512)}, u32[]{:S(2)}) copy-start(f32[512]{0:T(512)} %copy-done.28) | copy-start | bytes 6148
  879.9 82.7 %copy-start.32 = (f32[512]{0:T(512)S(1)}, f32[512]{0:T(512)}, u32[]{:S(2)}) copy-start(f32[512]{0:T(512)} %copy-done.31) | copy-start | bytes 6148
  879.9 259.8 %reduce-scatter.23.cloned.1.call-start = ((), (), s32[]{:S(2)}) async-start(), calls=%async_computation.20 | async-start | bytes 2654208 | tf_op jit(solution)/shard_map/reduce_scatter | solution.py:273
  887.1 75.5 %copy-start.5 = (f32[512,768]{1,0:T(8,128)S(1)}, f32[512,768]{1,0:T(8,128)}, u32[]{:S(2)}) copy-start(f32[512,768]{1,0:T(8,128)} %copy-done.4) | copy-start | bytes 4718596
  887.1 77.7 %copy-start.34 = (f32[512]{0:T(512)S(1)}, f32[512]{0:T(512)}, u32[]{:S(2)}) copy-start(f32[512]{0:T(512)} %copy-done.33) | copy-start | bytes 6148
  887.2 252.6 %all-reduce.3.cloned.1.call-start = ((), (), s32[]{:S(2)}) async-start(), calls=%async_computation.18 | async-start | bytes 6144000 | tf_op jit(solution)/shard_map/psum | solution.py:288
  1048.0 95.4 %copy-start.1 = (bf16[1000,768]{1,0:T(8,128)(2,1)S(1)}, bf16[1000,768]{1,0:T(8,128)(2,1)}, u32[]{:S(2)}) copy-start(bf16[1000,768]{1,0:T(8,128)(2,1)} %param.23) | copy-start | bytes 4608004
  (40 other events, 101.3 us)
Sparse Core Ops, SparseCore 0:
  16.4 66.1 all-gather.6
  138.6 109.3 reduce-scatter.12
  464.4 63.9 all-gather.14
  662.5 64.0 all-gather.16
  853.2 109.3 reduce-scatter.18
  965.9 35.8 reduce-scatter.26
  1005.5 40.5 reduce-scatter.24
  1050.0 42.7 reduce-scatter.20
  1097.2 42.5 reduce-scatter.22
Sparse Core Ops, SparseCore 1:
  140.9 22.5 all-gather.10
  251.8 63.8 all-gather.8
  317.5 22.5 all-gather.12
  347.6 110.6 reduce-scatter.14
  545.9 109.3 reduce-scatter.16
  971.3 144.0 all-reduce.2
where the time goes:
time: 1160 us; the launch traced here: 1150 us
  waiting for transfers between devices  758 us (65%)
  matrix products  195 us (17%)
  blocking collectives  64 us (6%)
  other arithmetic  60.3 us (5%)
  local copies, waits for them, and re-layouts  54.3 us (5%)
  between operations  17 us (1%)
    reduce_scatter x1, waiting for transfers between devices, shards(): lax.psum_scatter(contract_cols(pre_grad, up_weight), 'mp', scatter_dimens...  109 us
    reduce_scatter x1, waiting for transfers between devices, shards(): lax.psum_scatter(jnp.dot(attended, out_weight, preferred_element_type=jnp...  109 us
    reduce_scatter x1, waiting for transfers between devices, shards(): lax.psum_scatter(jnp.dot(hidden_act, down_weight, preferred_element_type=...  108 us
    reduce_scatter x1, waiting for transfers between devices, shards(): lax.psum_scatter(jnp.einsum('cge,cde->gd', projected_grad, qkv_weight, pr...  75.4 us
    unnamed x17, waiting for transfers between devices  72.2 us
    all_gather x1, waiting for transfers between devices, shards(): lax.all_gather(middle_grad.astype(jnp.bfloat16), 'mp', axis=0, tiled=True)  64.1 us
    all_gather x1, waiting for transfers between devices, shards(): final_all = lax.all_gather(final_low, 'mp', axis=0, tiled=True)  63.7 us
    all_gather x1, waiting for transfers between devices, shards(): second_all = lax.all_gather(second_norm, 'mp', axis=0, tiled=True)  62.4 us
  transfers between devices with their start and end apart: 15, of which 13 were waited for; matrix products, arithmetic and copies ran while one was open for 7% of the time, Pallas kernels for 0%

commit v1 on v0

--- a/solution.py
+++ b/solution.py
@@ -214,7 +214,12 @@
     )
     final_low = final_grad.astype(jnp.bfloat16)
     _, gelu_back = jax.vjp(gelu_exact, hidden_pre)
-    final_all = lax.all_gather(final_low, "mp", axis=0, tiled=True)
+    ring = [final_low]
+    for hop in range(3):
+        ring.append(lax.ppermute(ring[-1], "mp", [(dev, (dev + 1) % 4) for dev in range(4)]))
+    final_all = jnp.roll(
+        jnp.concatenate(ring[::-1], axis=0), (lax.axis_index("mp") + 1) * ring[0].shape[0], axis=0
+    )
     down_grad_part = contract_rows(hidden_act, final_all)
     act_grad = contract_cols(final_all, down_weight)
     pre_grad = gelu_back(act_grad)[0].astype(jnp.bfloat16)

time: 1160 us -> 1160 us (level)
    all_gather x1 -> x0, waiting for transfers between devices: 63.7 us -> none  [shards(): final_all = lax.all_gather(final_low, 'mp', axis=0, tiled=True)]
    ppermute x0 -> x3, waiting for transfers between devices: none -> 59.3 us  [shards(): lax.ppermute(ring[-1], 'mp', [(dev, (dev + 1) % 4) for dev in range(4)])]
    unnamed x101 -> x117, local copies, waits for them, and re-layouts: 29.7 us -> 35.7 us
    unnamed x17 -> x16, waiting for transfers between devices: 72.2 us -> 71.9 us
  transfers between devices with their start and end apart: 15 -> 17, of which waited for: 13 -> 15; matrix products, arithmetic and copies ran while one was open for 7% -> 7% of each run, Pallas kernels for 0% -> 0%
where the time goes in v1:
time: 1160 us; the launch traced here: 1150 us
  waiting for transfers between devices  753 us (65%)
  matrix products  194 us (17%)
  blocking collectives  64 us (6%)
  local copies, waits for them, and re-layouts  60.2 us (5%)
  other arithmetic  59.5 us (5%)
  between operations  17.2 us (1%)
    reduce_scatter x1, waiting for transfers between devices, shards(): lax.psum_scatter(jnp.dot(attended, out_weight, preferred_element_type=jnp...  109 us
    reduce_scatter x1, waiting for transfers between devices, shards(): lax.psum_scatter(contract_cols(pre_grad, up_weight), 'mp', scatter_dimens...  109 us
    reduce_scatter x1, waiting for transfers between devices, shards(): lax.psum_scatter(jnp.dot(hidden_act, down_weight, preferred_element_type=...  108 us
    reduce_scatter x1, waiting for transfers between devices, shards(): lax.psum_scatter(jnp.einsum('cge,cde->gd', projected_grad, qkv_weight, pr...  75.2 us
    unnamed x16, waiting for transfers between devices  71.9 us
    all_gather x1, waiting for transfers between devices, shards(): lax.all_gather(middle_grad.astype(jnp.bfloat16), 'mp', axis=0, tiled=True)  63.9 us
    all_gather x1, waiting for transfers between devices, shards(): second_all = lax.all_gather(second_norm, 'mp', axis=0, tiled=True)  62.1 us
    ppermute x3, waiting for transfers between devices, shards(): lax.ppermute(ring[-1], 'mp', [(dev, (dev + 1) % 4) for dev in range(4)])  59.3 us
  transfers between devices with their start and end apart: 17, of which 15 were waited for; matrix products, arithmetic and copies ran while one was open for 7% of the time, Pallas kernels for 0%

profile of v1, /device:TPU:0, one launch (start us, length us, event | category | flops | bytes accessed | tf_op | source)
XLA Modules:
  0.0 1151.1 jit_solution(14676328201209627301)
XLA Ops:
  17.3 14.6 %all_gather.22 = bf16[3,768,192]{2,0,1:T(4,128)(2,1)S(1)} all-gather(bf16[3,96,192]{2,0,1:T(4,128)(2,1)S(1)} %copy.44), channel_id=1, replica_groups=mesh['dp'=8,'mp'=4] {'dp'}, dimensions={1}, use_global_device_ids=true | all-gather | bytes 995328 | tf_op jit(solution)/shard_map/all_gather | solution.py:161
  34.0 8.7 all_gather.23
  43.7 39.0 %all-gather.6.cloned.1.call-done = bf16[2048,768]{1,0:T(8,128)(2,1)} async-done(((bf16[512,768]{1,0:T(8,128)(2,1)}), bf16[2048,768]{1,0:T(8,128)(2,1)}) %all-gather.6.cloned.1.call-update) | async-done | bytes 3145744 | tf_op jit(solution)/shard_map/all_gather | solution.py:167
  91.1 40.3 %while.28 = (s32[]{:T(128)}, bf16[4,512,3,64]{1,3,2,0:T(8,128)(2,1)}, f32[4,3,512]{2,1,0:T(4,128)S(1)}, bf16[4,512,3,64]{1,3,2,0:T(8,128)(2,1)S(1)}, bf16[2048,3...) while((s32[]{:T(128)}, ...), condition=%wide.region_5.6_spmd.clone, body=%wide.region_2.5_spmd.clone.sunk | while | flops 843055616 | bytes 46270628 | solution.py:67
  139.1 108.9 %reduce-scatter.13.cloned.1.call-done = f32[512,768]{1,0:T(8,128)} async-done(((f32[2048,768]{1,0:T(8,128)}), f32[512,768]{1,0:T(8,128)}) %reduce-scatter.13.cloned.1.call-update) | async-done | bytes 1572880 | tf_op jit(solution)/shard_map/reduce_scatter | solution.py:186
  253.6 62.1 %all-gather.8.cloned.1.call-done = bf16[2048,768]{1,0:T(8,128)(2,1)} async-done(((bf16[512,768]{1,0:T(8,128)(2,1)}), bf16[2048,768]{1,0:T(8,128)(2,1)}) %all-gather.8.cloned.1.call-update) | async-done | bytes 3145744 | tf_op jit(solution)/shard_map/all_gather | solution.py:194
  315.7 19.0 %multiply_convert_fusion.1 = (bf16[2048,768]{1,0:T(8,128)(2,1)}, f32[2048,768]{1,0:T(8,128)}, f32[2048,768]{1,0:T(8,128)}) fusion(f32[768]{0:T(1024)S(1)} %dynamic_slice.33, bf16[2048,768]{1,0:T(8,128)(2,1)} %all-gather.8.cloned.1.call-done, bf16[768,768]{1,0:T(8,128)(2,1)} %all-gather.10.cloned.1.call-done), kind=kOutput, calls=%fused_computation.54 | convolution fusion | flops 2519728128 | bytes 20057088 | tf_op jit(solution)/shard_map/dot_general | solution.py:196
  334.7 5.4 all-gather.12.cloned.1.call-done
  340.1 7.5 fusion.89
  350.2 108.2 %reduce-scatter.15.cloned.1.call-done = f32[512,768]{1,0:T(8,128)} async-done(((f32[2048,768]{1,0:T(8,128)}), f32[512,768]{1,0:T(8,128)}) %reduce-scatter.15.cloned.1.call-update) | async-done | bytes 1572880 | tf_op jit(solution)/shard_map/reduce_scatter | solution.py:200
  465.0 19.5 %collective-permute-done = bf16[512,768]{1,0:T(8,128)(2,1)S(1)} collective-permute-done((bf16[512,768]{1,0:T(8,128)(2,1)S(1)}, bf16[512,768]{1,0:T(8,128)(2,1)S(1)}, u32[]{:S(2)}, u32[]{:S(2)}) %collective-permute-start) | collective-permute-done | bytes 786464 | tf_op jit(solution)/shard_map/ppermute | solution.py:219
  485.4 20.2 %collective-permute-done.1 = bf16[512,768]{1,0:T(8,128)(2,1)} collective-permute-done((bf16[512,768]{1,0:T(8,128)(2,1)S(1)}, bf16[512,768]{1,0:T(8,128)(2,1)}, u32[]{:S(2)}, u32[]{:S(2)}) %collective-permute-start.1) | collective-permute-done | bytes 786464 | tf_op jit(solution)/shard_map/ppermute | solution.py:219
  505.7 19.5 %collective-permute-done.2 = bf16[512,768]{1,0:T(8,128)(2,1)} collective-permute-done((bf16[512,768]{1,0:T(8,128)(2,1)}, bf16[512,768]{1,0:T(8,128)(2,1)}, u32[]{:S(2)}, u32[]{:S(2)}) %collective-permute-start.2) | collective-permute-done | bytes 786464 | tf_op jit(solution)/shard_map/ppermute | solution.py:219
  530.5 10.1 convert_reduce_fusion
  547.0 108.9 %reduce-scatter.17.cloned.1.call-done = f32[512,768]{1,0:T(8,128)} async-done(((f32[2048,768]{1,0:T(8,128)}), f32[512,768]{1,0:T(8,128)}) %reduce-scatter.17.cloned.1.call-update) | async-done | bytes 1572880 | tf_op jit(solution)/shard_map/reduce_scatter | solution.py:230
  663.2 63.9 %all-gather.14.cloned.1.call-done = bf16[2048,768]{1,0:T(8,128)(2,1)} async-done(((bf16[512,768]{1,0:T(8,128)(2,1)}), bf16[2048,768]{1,0:T(8,128)(2,1)}) %all-gather.14.cloned.1.call-update) | async-done | bytes 3145744 | tf_op jit(solution)/shard_map/all_gather | solution.py:236
  737.1 105.5 %while.29 = (s32[]{:T(128)}, f32[2048,3,64]{0,2,1:T(8,128)S(1)}, f32[2048,3,64]{0,2,1:T(8,128)}, bf16[4,512,3,64]{1,3,2,0:T(8,128)(2,1)}, bf16[4,512,3,64]{1,3,2...) while((s32[]{:T(128)}, f32[2048,3,64]{0,2,1:T(8,128)S(1)}, ...), condition=%wide.region_16.17_spmd.clone, body=%wide.region_14.16_spmd.clone.sunk | while | flops 2062516736 | bytes 129419448 | solution.py:114
  755.0 5.7 fusion.155
  766.4 5.5 fusion.154
  781.5 5.6 fusion.155
  792.9 5.5 fusion.154
  807.9 5.7 fusion.155
  819.3 5.5 fusion.154
  834.4 5.7 fusion.155
  858.6 5.6 fusion.62
  873.2 6.9 fusion.91
  880.5 6.9 fusion.53
  887.5 75.2 %reduce-scatter.19.cloned.1.call-done = f32[512,768]{1,0:T(8,128)} async-done(((f32[2048,768]{1,0:T(8,128)}), f32[512,768]{1,0:T(8,128)}) %reduce-scatter.19.cloned.1.call-update) | async-done | bytes 1572880 | tf_op jit(solution)/shard_map/reduce_scatter | solution.py:265
  973.7 28.2 %reduce-scatter.27.cloned.1.call-done = f32[96,192]{1,0:T(8,128)} async-done(((f32[768,192]{1,0:T(8,128)}), f32[96,192]{1,0:T(8,128)}) %reduce-scatter.27.cloned.1.call-update) | async-done | bytes 73744
  1003.5 42.5 %reduce-scatter.25.cloned.1.call-done = f32[96,576]{1,0:T(8,128)} async-done(((f32[768,576]{1,0:T(8,128)}), f32[96,576]{1,0:T(8,128)}) %reduce-scatter.25.cloned.1.call-update) | async-done | bytes 221200
  1047.9 40.6 %all-reduce = (f32[8,768]{1,0:T(8,128)S(1)}, f32[3072]{0:T(1024)}) all-reduce(f32[8,768]{1,0:T(8,128)S(1)} %stack.37, f32[3072]{0:T(1024)S(1)} %dynamic_update_slice.18), channel_id=1, replica_groups=mesh['dp'=8,'mp'=4] {'dp','mp'}, use_global_device_ids=true, to_apply=%region_28.29 | all-reduce | flops 9216 | bytes 73728 | tf_op jit(solution)/shard_map/psum | solution.py:293
  1093.1 46.7 %reduce-scatter.23.cloned.1.call-done = f32[768,96]{0,1:T(8,128)} async-done(((f32[768,768]{0,1:T(8,128)}), f32[768,96]{0,1:T(8,128)}) %reduce-scatter.23.cloned.1.call-update) | async-done | bytes 294928 | tf_op jit(solution)/shard_map/reduce_scatter | solution.py:278
  (294 shorter events, 226.0 us)
Async XLA Ops:
  8.0 74.7 %all-gather.6.cloned.1.call-start = ((), (), s32[]{:S(2)}) async-start(), calls=%async_computation.8 | async-start | bytes 3932160 | tf_op jit(solution)/shard_map/all_gather | solution.py:167
  16.3 231.7 %reduce-scatter.13.cloned.1.call-start = ((), (), s32[]{:S(2)}) async-start(), calls=%async_computation.9 | async-start | bytes 7864320 | tf_op jit(solution)/shard_map/reduce_scatter | solution.py:186
  131.3 7.1 copy-start.3
  131.3 7.1 copy-start.9
  138.5 109.6 %copy-start.45 = (f32[768]{0:T(1024)S(1)}, f32[768]{0:T(1024)}, u32[]{:S(2)}) copy-start(f32[768]{0:T(1024)} %param.29) | copy-start | bytes 9220
  138.5 115.1 %all-gather.10.cloned.1.call-start = ((), (), s32[]{:S(2)}) async-start(), calls=%async_computation.11 | async-start | bytes 1327104 | tf_op jit(solution)/shard_map/all_gather | solution.py:163
  139.1 176.7 %all-gather.8.cloned.1.call-start = ((), (), s32[]{:S(2)}) async-start(), calls=%async_computation.10 | async-start | bytes 3932160 | tf_op jit(solution)/shard_map/all_gather | solution.py:194
  251.7 88.3 %all-gather.12.cloned.1.call-start = ((), (), s32[]{:S(2)}) async-start(), calls=%async_computation.12 | async-start | bytes 1327104 | tf_op jit(solution)/shard_map/all_gather | solution.py:164
  252.3 206.1 %reduce-scatter.15.cloned.1.call-start = ((), (), s32[]{:S(2)}) async-start(), calls=%async_computation.13 | async-start | bytes 7864320 | tf_op jit(solution)/shard_map/reduce_scatter | solution.py:200
  347.6 110.8 %copy-start.46 = (f32[768]{0:T(1024)S(1)}, f32[768]{0:T(1024)}, u32[]{:S(2)}) copy-start(f32[768]{0:T(1024)} %param.33) | copy-start | bytes 9220
  347.6 308.2 %reduce-scatter.17.cloned.1.call-start = ((), (), s32[]{:S(2)}) async-start(), calls=%async_computation.14 | async-start | bytes 7864320 | tf_op jit(solution)/shard_map/reduce_scatter | solution.py:230
  463.5 21.1 %collective-permute-start = (bf16[512,768]{1,0:T(8,128)(2,1)S(1)}, bf16[512,768]{1,0:T(8,128)(2,1)S(1)}, u32[]{:S(2)}, u32[]{:S(2)}) collective-permute-start(bf16[512,768]{1,0:T(8,128)(2,1)S(1)} %convert_element_type.78), channel_id=1, source_target_pairs={{0,1},{1,2},{2,3},{3,0},{4,5},{5,6},{6,7},{7,4},{8,9},{9,10},{10,1... | collective-permute-start | bytes 2359304 | tf_op jit(solution)/shard_map/ppermute | solution.py:219
  485.4 20.2 %collective-permute-start.1 = (bf16[512,768]{1,0:T(8,128)(2,1)S(1)}, bf16[512,768]{1,0:T(8,128)(2,1)}, u32[]{:S(2)}, u32[]{:S(2)}) collective-permute-start(bf16[512,768]{1,0:T(8,128)(2,1)S(1)} %collective-permute-done), channel_id=1, source_target_pairs={{0,1},{1,2},{2,3},{3,0},{4,5},{5,6},{6,7},{7,4},{8,9},{9,10},{10,1... | collective-permute-start | bytes 2359304 | tf_op jit(solution)/shard_map/ppermute | solution.py:219
  505.7 19.5 %collective-permute-start.2 = (bf16[512,768]{1,0:T(8,128)(2,1)}, bf16[512,768]{1,0:T(8,128)(2,1)}, u32[]{:S(2)}, u32[]{:S(2)}) collective-permute-start(bf16[512,768]{1,0:T(8,128)(2,1)} %collective-permute-done.1), channel_id=1, source_target_pairs={{0,1},{1,2},{2,3},{3,0},{4,5},{5,6},{6,7},{7,4},{8,9},{9,10},{10,1... | collective-permute-start | bytes 2359304 | tf_op jit(solution)/shard_map/ppermute | solution.py:219
  505.7 21.9 %copy-start.18 = (bf16[512,768]{1,0:T(8,128)(2,1)S(1)}, bf16[512,768]{1,0:T(8,128)(2,1)}, u32[]{:S(2)}) copy-start(bf16[512,768]{1,0:T(8,128)(2,1)} %copy-done.17) | copy-start | bytes 2359300
  505.7 22.0 %copy-start.5 = (f32[512,768]{1,0:T(8,128)S(1)}, f32[512,768]{1,0:T(8,128)}, u32[]{:S(2)}) copy-start(f32[512,768]{1,0:T(8,128)} %copy-done.4) | copy-start | bytes 4718596
  530.4 10.2 copy-start.29
  530.5 11.8 %copy-start.48 = (bf16[768,768]{1,0:T(8,128)(2,1)S(1)}, bf16[768,768]{1,0:T(8,128)(2,1)}, u32[]{:S(2)}) copy-start(bf16[768,768]{1,0:T(8,128)(2,1)} %all-gather.10.cloned.1.call-done) | copy-start | bytes 3538948
  546.7 180.3 %all-gather.14.cloned.1.call-start = ((), (), s32[]{:S(2)}) async-start(), calls=%async_computation.15 | async-start | bytes 3932160 | tf_op jit(solution)/shard_map/all_gather | solution.py:236
  663.1 299.6 %reduce-scatter.19.cloned.1.call-start = ((), (), s32[]{:S(2)}) async-start(), calls=%async_computation.16 | async-start | bytes 7864320 | tf_op jit(solution)/shard_map/reduce_scatter | solution.py:265
  834.4 5.7 copy-start.2
  853.3 148.6 %reduce-scatter.27.cloned.1.call-start = ((), (), s32[]{:S(2)}) async-start(), calls=%async_computation.21 | async-start | bytes 884736
  858.5 187.4 %reduce-scatter.25.cloned.1.call-start = ((), (), s32[]{:S(2)}) async-start(), calls=%async_computation.20 | async-start | bytes 2211840
  873.2 219.9 %reduce-scatter.21.cloned.1.call-start = ((), (), s32[]{:S(2)}) async-start(), calls=%async_computation.18 | async-start | bytes 2654208 | tf_op jit(solution)/shard_map/reduce_scatter | solution.py:277
  880.2 82.5 %copy-start.31 = (f32[768]{0:T(1024)S(1)}, f32[768]{0:T(1024)}, u32[]{:S(2)}) copy-start(f32[768]{0:T(1024)} %copy-done.30) | copy-start | bytes 9220
  880.2 82.5 %copy-start.33 = (f32[512]{0:T(512)S(1)}, f32[512]{0:T(512)}, u32[]{:S(2)}) copy-start(f32[512]{0:T(512)} %copy-done.32) | copy-start | bytes 6148
  880.2 82.5 %copy-start.36 = (f32[512]{0:T(512)S(1)}, f32[512]{0:T(512)}, u32[]{:S(2)}) copy-start(f32[512]{0:T(512)} %copy-done.35) | copy-start | bytes 6148
  880.2 259.6 %reduce-scatter.23.cloned.1.call-start = ((), (), s32[]{:S(2)}) async-start(), calls=%async_computation.19 | async-start | bytes 2654208 | tf_op jit(solution)/shard_map/reduce_scatter | solution.py:278
  887.4 75.3 %copy-start.8 = (f32[512,768]{1,0:T(8,128)S(1)}, f32[512,768]{1,0:T(8,128)}, u32[]{:S(2)}) copy-start(f32[512,768]{1,0:T(8,128)} %copy-done.7) | copy-start | bytes 4718596
  887.4 77.5 %copy-start.38 = (f32[512]{0:T(512)S(1)}, f32[512]{0:T(512)}, u32[]{:S(2)}) copy-start(f32[512]{0:T(512)} %copy-done.37) | copy-start | bytes 6148
  887.4 252.3 %all-reduce.3.cloned.1.call-start = ((), (), s32[]{:S(2)}) async-start(), calls=%async_computation.17 | async-start | bytes 6144000 | tf_op jit(solution)/shard_map/psum | solution.py:293
  1047.9 95.6 %copy-start.1 = (bf16[1000,768]{1,0:T(8,128)(2,1)S(1)}, bf16[1000,768]{1,0:T(8,128)(2,1)}, u32[]{:S(2)}) copy-start(bf16[1000,768]{1,0:T(8,128)(2,1)} %param.23) | copy-start | bytes 4608004
  (47 other events, 131.5 us)
Sparse Core Ops, SparseCore 0:
  16.4 66.1 all-gather.5
  138.6 109.3 reduce-scatter.12
  546.9 108.9 reduce-scatter.16
  971.4 144.0 all-reduce.2
Sparse Core Ops, SparseCore 1:
  140.8 22.5 all-gather.9
  251.8 63.8 all-gather.7
  317.5 22.5 all-gather.11
  347.7 110.6 reduce-scatter.14
  663.2 63.8 all-gather.13
  853.3 109.3 reduce-scatter.18
  966.0 35.8 reduce-scatter.26
  1005.5 40.4 reduce-scatter.24
  1049.8 43.2 reduce-scatter.20
  1097.4 42.4 reduce-scatter.22
